TPU v7x, 256 devices: a whole 4x4x8 slice. The times are simulated.
256 devices in a mesh: slab: 16 (over x, y), pencil: 16 (over z, core).
Axes of the slice: x: 4, y: 4, z: 8, core: 2. Of those that a mesh axis runs over, the one named last changes fastest.
Arguments:
- charges: bfloat16 [64, 131072], P(None, ('slab', 'pencil')), may hold values from -6 to 6
- cotangent: bfloat16 [64, 131072], P(None, ('slab', 'pencil')), may hold values from -6 to 6
- base_cell: int32 [3, 131072], P(None, ('slab', 'pencil')), may hold values from 0 to 63, as said below
- frac: float32 [3, 131072], P(None, ('slab', 'pencil')), may hold values from 0 to 1
- counts: int32 [256], P(('slab', 'pencil')), may hold values from 256 to 512, as said below
- filter_weights: float32 [32, 64], replicated, may hold values from -6 to 6
Outputs:
- potential: bfloat16 [64, 131072], P(None, ('slab', 'pencil'))
- charge_grad: bfloat16 [64, 131072], P(None, ('slab', 'pencil'))
- filter_grad: float32 [32, 64], replicated
Inputs may be any that keep to these rules, and one draw needn't show every extreme that they name: `base_cell`: slots d * 512 to (d + 1) * 512 - 1 belong to device d = slab index * (pencil axis size) + pencil index; their first cell index lies in the slab index's run of 4 cells and their second in the pencil index's run of 4 cells; the third is any cell. A device's live atoms are its first counts slots; some device's count is 512.
All inputs are finite; a program needn't handle non-finite values.
Results may differ from a plain program's by a relative error of at most 0.013.
Values may be sent and summed in bfloat16 or wider, within the bound.
A program may use at most 128 MiB of HBM per device.

v0:
```python
import jax
import jax.numpy as jnp
from jax import lax
from jax.sharding import PartitionSpec as P

N = 64
C = 64
NB = 32
ENV_SCALE = 40.0
ENV_WIDTH = 16.0


def passed_along(value, axis, steps):
    count = lax.axis_size(axis)
    pairs = [(source, (source + steps) % count) for source in range(count)]
    return lax.ppermute(value, axis, pairs)


def spline_weights(frac):
    remain = 1.0 - frac
    square = frac * frac
    cubed = square * frac
    weight_zero = remain * remain * remain / 6.0
    weight_one = (3.0 * cubed - 6.0 * square + 4.0) / 6.0
    weight_two = (-3.0 * cubed + 3.0 * square + 3.0 * frac + 1.0) / 6.0
    weight_three = cubed / 6.0
    return jnp.stack([weight_zero, weight_one, weight_two, weight_three], axis=1)


def stencil_local(base_cell, frac, live, x_first, y_first, span_y):
    weights = spline_weights(frac)
    offsets = jnp.arange(64, dtype=jnp.int32)
    along_x = jnp.repeat(weights[0], 16, axis=0)
    along_y = jnp.tile(jnp.repeat(weights[1], 4, axis=0), (4, 1))
    along_z = jnp.tile(weights[2], (16, 1))
    stencil = along_x * along_y * along_z * live[None, :]
    local_x = base_cell[0][None, :] - x_first + offsets[:, None] // 16
    local_y = base_cell[1][None, :] - y_first + offsets[:, None] // 4 % 4
    local_z = (base_cell[2][None, :] + offsets[:, None] % 4) % N
    cell_ids = (local_x * (span_y + 3) + local_y) * N + local_z
    return (cell_ids, stencil)


def frequencies(positions):
    return jnp.where(positions < N // 2, positions, positions - N).astype(jnp.float32)


def filter_shells(y_first, z_first, y_count, z_count):
    freq_x = frequencies(jnp.arange(N, dtype=jnp.int32))
    freq_y = frequencies(y_first + jnp.arange(y_count, dtype=jnp.int32))
    freq_z = frequencies(z_first + jnp.arange(z_count, dtype=jnp.int32))
    kappa_sq = (
        freq_x[:, None, None] * freq_x[:, None, None]
        + freq_y[None, :, None] * freq_y[None, :, None]
        + freq_z[None, None, :] * freq_z[None, None, :]
    )
    kappa = jnp.sqrt(kappa_sq)
    envelope = ENV_SCALE * ENV_WIDTH / (ENV_WIDTH + kappa_sq)
    spacing = N / (2.0 * NB)
    centers = (jnp.arange(NB, dtype=jnp.float32) + 0.5) * spacing
    shells = envelope[..., None] * jnp.exp(-jnp.square((kappa[..., None] - centers) / spacing))
    return shells.reshape(N * y_count * z_count, NB)


def dft_tables(length):
    indices = jnp.arange(length, dtype=jnp.int32)
    phases = indices[:, None] * indices[None, :] % length
    angles = phases.astype(jnp.float32) * (2.0 * jnp.pi / length)
    return (jnp.cos(angles), jnp.sin(angles))


def contract(operand, matrix, pattern):
    if operand.dtype == jnp.bfloat16:
        table_high = matrix.astype(jnp.bfloat16)
        table_low = (matrix - table_high.astype(jnp.float32)).astype(jnp.bfloat16)
        first = jnp.einsum(pattern, operand, table_high, preferred_element_type=jnp.float32)
        second = jnp.einsum(pattern, operand, table_low, preferred_element_type=jnp.float32)
        return first + second
    return jnp.einsum(pattern, operand, matrix, precision=lax.Precision.HIGHEST)


def transform(values, pattern, inverse, real_in, real_out):
    cosines, sines = dft_tables(N)
    direction = 1.0 if inverse else -1.0
    factor = 1.0 / N if inverse else 1.0
    if real_in:
        real_part = values
        new_real = contract(real_part, cosines, pattern)
        new_imag = direction * contract(real_part, sines, pattern)
    else:
        halfway = values.shape[-1] // 2
        real_part = values[..., :halfway]
        imag_part = values[..., halfway:]
        new_real = contract(real_part, cosines, pattern) - direction * contract(
            imag_part, sines, pattern
        )
        if real_out:
            return new_real * factor
        new_imag = contract(imag_part, cosines, pattern) + direction * contract(
            real_part, sines, pattern
        )
    return jnp.concatenate([new_real, new_imag], axis=-1) * factor


def spread(values, cell_ids, stencil, span_x, span_y, blocks_run):
    channels = values.shape[1]
    total_cells = (span_x + 3) * (span_y + 3) * N

    def add_block(number, totals):
        block_vals = values.astype(jnp.float32)
        products = stencil[:, :, None] * block_vals[None, :, :]
        return totals.at[cell_ids.reshape(-1)].add(products.reshape(-1, channels))

    totals = lax.fori_loop(
        0, blocks_run, add_block, jnp.zeros((total_cells, channels), jnp.float32)
    )
    totals = totals.reshape(span_x + 3, span_y + 3, N, channels)
    rim_planes = passed_along(totals[span_x:].astype(jnp.bfloat16), "slab", 1).astype(jnp.float32)
    totals = totals[:span_x].at[:3].add(rim_planes)
    rim_rows = passed_along(totals[:, span_y:].astype(jnp.bfloat16), "pencil", 1).astype(
        jnp.float32
    )
    return totals[:, :span_y].at[:, :3].add(rim_rows)


def interpolate(grid_vals, cell_ids, stencil, blocks_run, block_len, slots):
    ghost_planes = passed_along(grid_vals[:3], "slab", -1)
    grid_vals = jnp.concatenate([grid_vals, ghost_planes], axis=0)
    ghost_rows = passed_along(grid_vals[:, :3], "pencil", -1)
    grid_vals = jnp.concatenate([grid_vals, ghost_rows], axis=1)
    channels = grid_vals.shape[3]
    flattened = grid_vals.reshape(-1, channels)

    def take_block(number, result):
        picked = (
            flattened[cell_ids.reshape(-1)].reshape(64, block_len, channels).astype(jnp.float32)
        )
        summed = jnp.sum(stencil[:, :, None] * picked, axis=0).astype(jnp.bfloat16)
        return summed

    return lax.fori_loop(0, blocks_run, take_block, jnp.zeros((slots, channels), jnp.bfloat16))


def forward_spectrum(density):
    section_one = transform(density, "xyzc,zk->xykc", False, True, False).astype(jnp.bfloat16)

    def along_y(block_vals):
        return transform(block_vals, "xyzc,yk->xkzc", False, False, False).astype(jnp.bfloat16)

    middle = along_y(lax.all_to_all(section_one, "pencil", split_axis=2, concat_axis=1, tiled=True))

    def along_x(block_vals):
        return transform(block_vals, "xyzc,xk->kyzc", False, False, False)

    return along_x(lax.all_to_all(middle, "slab", split_axis=1, concat_axis=0, tiled=True))


def back_to_cells(spectrum):
    section_one = transform(spectrum, "xyzc,xk->kyzc", True, False, False).astype(jnp.bfloat16)

    def along_y(block_vals):
        return transform(block_vals, "xyzc,yk->xkzc", True, False, False).astype(jnp.bfloat16)

    middle = along_y(lax.all_to_all(section_one, "slab", split_axis=0, concat_axis=1, tiled=True))

    def along_z(block_vals):
        return transform(block_vals, "xyzc,zk->xykc", True, False, True).astype(jnp.bfloat16)

    return along_z(lax.all_to_all(middle, "pencil", split_axis=1, concat_axis=2, tiled=True))


def per_device(charges, cotangent, base_cell, frac, counts, filter_weights):
    charges = charges.T
    cotangent = cotangent.T
    slab_index = lax.axis_index("slab")
    pencil_index = lax.axis_index("pencil")
    span_x = N // lax.axis_size("slab")
    span_y = N // lax.axis_size("pencil")
    slots = charges.shape[0]
    block_len = min(512, slots)
    live_count = counts[0]
    live = (jnp.arange(slots, dtype=jnp.int32) < live_count).astype(jnp.float32)
    cell_ids, stencil = stencil_local(
        base_cell, frac, live, slab_index * span_x, pencil_index * span_y, span_y
    )
    blocks_run = slots // block_len
    shells = filter_shells(slab_index * span_x, pencil_index * span_y, span_x, span_y)
    profile = jnp.dot(shells, filter_weights, precision=lax.Precision.HIGHEST).reshape(
        N, span_x, span_y, C
    )
    doubled = jnp.tile(profile, (1, 1, 1, 2))
    spectrum_q = forward_spectrum(spread(charges, cell_ids, stencil, span_x, span_y, blocks_run))
    potential = interpolate(
        back_to_cells(spectrum_q * doubled), cell_ids, stencil, blocks_run, block_len, slots
    )
    spectrum_g = forward_spectrum(spread(cotangent, cell_ids, stencil, span_x, span_y, blocks_run))
    correlation = (
        spectrum_g[..., :C] * spectrum_q[..., :C] + spectrum_g[..., C:] * spectrum_q[..., C:]
    )
    charge_grad = interpolate(
        back_to_cells(spectrum_g * doubled), cell_ids, stencil, blocks_run, block_len, slots
    )
    partial_grad = jnp.dot(
        shells.T, correlation.reshape(-1, C), precision=lax.Precision.HIGHEST
    ) / (N * N * N)
    filter_grad = lax.psum(partial_grad, ("slab", "pencil"))
    return (potential.T, charge_grad.T, filter_grad)


def solution(mesh):
    in_specs = (
        P(None, ("slab", "pencil")),
        P(None, ("slab", "pencil")),
        P(None, ("slab", "pencil")),
        P(None, ("slab", "pencil")),
        P(("slab", "pencil")),
        P(),
    )
    out_specs = (P(None, ("slab", "pencil")), P(None, ("slab", "pencil")), P())
    return jax.shard_map(
        per_device, mesh=mesh, in_specs=in_specs, out_specs=out_specs, check_vma=False
    )
```

profile of v0, /device:TPU:1, one launch (start us, length us, event | category | flops | bytes accessed | tf_op | source)
XLA Modules:
  0.0 876.0 jit_solution(3839491875228261354)
XLA Ops:
  6.2 12.0 %bitcast_multiply_fusion.1 = (f32[32768,64]{1,0:T(8,128)}, f32[32768,64]{1,0:T(8,128)}) fusion(f32[512,64]{1,0:T(8,128)S(1)} %copy.19, f32[32768]{0:T(1024)S(1)} %multiply_multiply_fusion, f32[512,64]{1,0:T(8,128)S(1)} %copy.28), kind=kLoop, calls=%fused_computation.9 | loop fusion | flops 4194304 | bytes 17170432 | tf_op jit(solution)/shard_map/while/body/eval_jaxpr/mul | solution.py:111
  18.2 174.7 %scatter_custom_fusion.1 = f32[3136,64]{1,0:T(8,128)S(1)} fusion(s32[32768]{0:T(1024)S(1)} %bitcast.346, f32[32768,64]{1,0:T(8,128)} %get-tuple-element.117, f32[]{:T(128)} %constant.266.clone.1), kind=kCustom, calls=%fused_computation.96 | custom fusion | flops 2097152 | bytes 803328 | tf_op jit(solution)/shard_map/while/body/eval_jaxpr/scatter-add | solution.py:112
  193.6 2.1 collective-permute-start.4
  195.8 174.7 %scatter_custom_fusion = f32[3136,64]{1,0:T(8,128)S(1)} fusion(s32[32768]{0:T(1024)S(1)} %bitcast.347, f32[32768,64]{1,0:T(8,128)} %get-tuple-element.116, f32[]{:T(128)} %constant.266.clone.1), kind=kCustom, calls=%fused_computation.98 | custom fusion | flops 2097152 | bytes 803328 | tf_op jit(solution)/shard_map/while/body/eval_jaxpr/scatter-add | solution.py:112
  371.2 1.8 collective-permute-start
  380.6 2.1 add_dynamic-update-slice_fusion
  383.7 2.8 collective-permute-start.5
  393.4 9.9 %all-to-all-start.4 = ((bf16[4,4,64,128]{3,1,0,2:T(4,128)(2,1)}), bf16[4,4,64,128]{3,1,0,2:T(4,128)(2,1)S(1)}, u32[]{:S(2)}, u32[]{:S(2)}) async-start(bf16[4,4,64,128]{3,1,0,2:T(4,128)(2,1)} %copy.29), calls=%async_computation.4 | async-start | bytes 524288 | tf_op jit(solution)/shard_map/all_to_all | solution.py:150
  406.8 8.1 all-to-all-done.4
  414.9 3.4 all-to-all-start
  421.5 8.0 all-to-all-done
  437.2 6.0 all-to-all-start.5
  447.9 3.2 all-to-all-done.5
  451.1 3.9 all-to-all-start.1
  457.3 5.1 all-to-all-done.1
  474.7 4.4 all-to-all-start.2
  479.1 1.8 convolution_subtract_fusion
  482.7 3.8 all-to-all-done.2
  486.5 3.6 all-to-all-start.6
  495.8 1.6 all-to-all-done.6
  506.9 8.0 all-to-all-start.3
  520.0 6.7 all-to-all-done.3
  526.7 3.4 all-to-all-start.7
  530.2 1.6 fusion.161
  533.4 7.7 all-to-all-done.7
  543.7 2.3 collective-permute-start.2
  547.7 2.7 collective-permute-done.2
  551.6 2.9 collective-permute-done.6
  558.1 76.5 %psum.7 = f32[32,64]{1,0:T(8,128)} all-reduce(f32[32,64]{1,0:T(8,128)S(1)} %fusion.48), channel_id=1, replica_groups=mesh['slab'=16,'pencil'=16] {'slab','pencil'}, use_global_device_ids=true, to_apply=%region_4.5 | all-reduce | flops 2048 | bytes 16384 | tf_op jit(solution)/shard_map/psum | solution.py:206
  635.7 114.9 %gather_fusion = bf16[32768,64]{1,0:T(8,128)(2,1)} fusion(bf16[3136,64]{1,0:T(8,128)(2,1)S(1)} %bitcast.273, s32[32768]{0:T(1024)S(1)} %broadcast_clamp_fusion), kind=kCustom, calls=%fused_computation | custom fusion | bytes 8519680 | tf_op jit(solution)/shard_map/while/body/eval_jaxpr/gather | solution.py:136
  751.8 114.9 %gather_fusion.1 = bf16[32768,64]{1,0:T(8,128)(2,1)} fusion(bf16[3136,64]{1,0:T(8,128)(2,1)S(1)} %bitcast.272, s32[32768]{0:T(1024)S(1)} %broadcast_clamp_fusion), kind=kCustom, calls=%fused_computation.1 | custom fusion | bytes 8519680 | tf_op jit(solution)/shard_map/while/body/eval_jaxpr/gather | solution.py:136
  866.7 7.5 fusion
  (189 shorter events, 91.3 us)
Async XLA Ops:
  0.6 376.4 %copy-start = (f32[32,64]{1,0:T(8,128)S(1)}, f32[32,64]{1,0:T(8,128)}, u32[]{:S(2)}) copy-start(f32[32,64]{1,0:T(8,128)} %param.19) | copy-start | bytes 24580
  1.4 0.9 copy-start.10
  2.3 15.9 %copy-start.11 = (f32[512]{0:T(512)}, f32[512]{0:T(512)S(1)}, u32[]{:S(2)}) copy-start(f32[512]{0:T(512)S(1)} %fusion.301) | copy-start | bytes 6148
  6.1 189.7 %copy-start.5 = (s32[32768,1]{0,1:T(1,128)}, s32[32768,1]{0,1:T(1,128)S(1)}, u32[]{:S(2)}) copy-start(s32[32768,1]{0,1:T(1,128)S(1)} %compare_select_fusion) | copy-start | bytes 393220
  193.6 186.9 %collective-permute-start.4 = (bf16[3,7,64,64]{3,2,1,0:T(8,128)(2,1)}, bf16[3,7,64,64]{3,2,1,0:T(8,128)(2,1)}, u32[]{:S(2)}, u32[]{:S(2)}) collective-permute-start(bf16[3,7,64,64]{3,2,1,0:T(8,128)(2,1)} %bitcast.66), channel_id=1, source_target_pairs={{0,16},{16,32},{32,48},{48,64},{64,80},{80,96},{96,112},{112,128},... | collective-permute-start | bytes 516104 | tf_op jit(solution)/shard_map/ppermute | solution.py:16
  371.2 15.2 %collective-permute-start = (bf16[3,7,64,64]{3,2,1,0:T(8,128)(2,1)}, bf16[3,7,64,64]{3,2,1,0:T(8,128)(2,1)}, u32[]{:S(2)}, u32[]{:S(2)}) collective-permute-start(bf16[3,7,64,64]{3,2,1,0:T(8,128)(2,1)} %bitcast.21), channel_id=1, source_target_pairs={{0,16},{16,32},{32,48},{48,64},{64,80},{80,96},{96,112},{112,128},... | collective-permute-start | bytes 516104 | tf_op jit(solution)/shard_map/ppermute | solution.py:16
  375.9 29.1 %copy-start.13 = (f32[32]{0:T(128)}, f32[32]{0:T(128)S(1)}, u32[]{:S(2)}) copy-start(f32[32]{0:T(128)S(1)} %iota_add_fusion) | copy-start | bytes 388
  377.0 28.7 %copy-start.6 = (f32[64,4,4]{0,2,1:T(4,128)}, f32[64,4,4]{0,2,1:T(4,128)S(1)}, u32[]{:S(2)}) copy-start(f32[64,4,4]{0,2,1:T(4,128)S(1)} %get-tuple-element.128) | copy-start | bytes 12292
  377.0 28.7 %copy-start.8 = (f32[64,4,4]{0,2,1:T(4,128)}, f32[64,4,4]{0,2,1:T(4,128)S(1)}, u32[]{:S(2)}) copy-start(f32[64,4,4]{0,2,1:T(4,128)S(1)} %get-tuple-element.129) | copy-start | bytes 12292
  383.7 6.1 collective-permute-start.5
  388.9 14.4 %collective-permute-start.1 = (bf16[4,3,64,64]{3,2,1,0:T(8,128)(2,1)S(1)}, bf16[4,3,64,64]{3,2,1,0:T(8,128)(2,1)}, u32[]{:S(2)}, u32[]{:S(2)}) collective-permute-start(bf16[4,3,64,64]{3,2,1,0:T(8,128)(2,1)S(1)} %slice.473), channel_id=1, source_target_pairs={{0,1},{1,2},{2,3},{3,4},{4,5},{5,6},{6,7},{7,8},{8,9},{9,10},{10,1... | collective-permute-start | bytes 294920 | tf_op jit(solution)/shard_map/ppermute | solution.py:16
  393.4 21.5 %all-to-all-start.4 = ((bf16[4,4,64,128]{3,1,0,2:T(4,128)(2,1)}), bf16[4,4,64,128]{3,1,0,2:T(4,128)(2,1)S(1)}, u32[]{:S(2)}, u32[]{:S(2)}) async-start(bf16[4,4,64,128]{3,1,0,2:T(4,128)(2,1)} %copy.29), calls=%async_computation.4 | async-start | bytes 524288 | tf_op jit(solution)/shard_map/all_to_all | solution.py:150
  414.9 14.6 %all-to-all-start = ((bf16[4,4,64,128]{3,1,0,2:T(4,128)(2,1)}), bf16[4,4,64,128]{3,1,0,2:T(4,128)(2,1)S(1)}, u32[]{:S(2)}, u32[]{:S(2)}) async-start(bf16[4,4,64,128]{3,1,0,2:T(4,128)(2,1)} %copy.20), calls=%async_computation | async-start | bytes 524288 | tf_op jit(solution)/shard_map/all_to_all | solution.py:150
  437.2 13.9 %all-to-all-start.5 = ((bf16[4,64,4,128]{3,2,0,1:T(4,128)(2,1)}), bf16[4,64,4,128]{3,2,0,1:T(4,128)(2,1)S(1)}, u32[]{:S(2)}, u32[]{:S(2)}) async-start(bf16[4,64,4,128]{3,2,0,1:T(4,128)(2,1)} %copy.31), calls=%async_computation.5 | async-start | bytes 524288 | tf_op jit(solution)/shard_map/all_to_all | solution.py:155
  451.1 11.3 %all-to-all-start.1 = ((bf16[4,64,4,128]{3,2,0,1:T(4,128)(2,1)}), bf16[4,64,4,128]{3,2,0,1:T(4,128)(2,1)S(1)}, u32[]{:S(2)}, u32[]{:S(2)}) async-start(bf16[4,64,4,128]{3,2,0,1:T(4,128)(2,1)} %copy.22), calls=%async_computation.1 | async-start | bytes 524288 | tf_op jit(solution)/shard_map/all_to_all | solution.py:155
  474.7 11.9 %all-to-all-start.2 = ((bf16[64,4,4,128]{3,2,1,0:T(4,128)(2,1)}), bf16[64,4,4,128]{3,2,1,0:T(4,128)(2,1)}, u32[]{:S(2)}, u32[]{:S(2)}) async-start(bf16[64,4,4,128]{3,2,1,0:T(4,128)(2,1)} %copy.24), calls=%async_computation.2 | async-start | bytes 524288 | tf_op jit(solution)/shard_map/all_to_all | solution.py:164
  486.5 10.9 %all-to-all-start.6 = ((bf16[64,4,4,128]{3,2,1,0:T(4,128)(2,1)}), bf16[64,4,4,128]{3,2,1,0:T(4,128)(2,1)S(1)}, u32[]{:S(2)}, u32[]{:S(2)}) async-start(bf16[64,4,4,128]{3,2,1,0:T(4,128)(2,1)} %copy.33), calls=%async_computation.6 | async-start | bytes 524288 | tf_op jit(solution)/shard_map/all_to_all | solution.py:164
  501.6 28.6 %copy-start.12 = (f32[512]{0:T(512)S(1)}, f32[512]{0:T(512)}, u32[]{:S(2)}) copy-start(f32[512]{0:T(512)} %copy-done.11) | copy-start | bytes 6148
  506.9 19.8 %all-to-all-start.3 = ((bf16[4,64,4,128]{3,2,0,1:T(4,128)(2,1)}), bf16[4,64,4,128]{3,2,0,1:T(4,128)(2,1)S(1)}, u32[]{:S(2)}, u32[]{:S(2)}) async-start(bf16[4,64,4,128]{3,2,0,1:T(4,128)(2,1)} %copy.26), calls=%async_computation.3 | async-start | bytes 524288 | tf_op jit(solution)/shard_map/all_to_all | solution.py:169
  518.5 38.3 %copy-start.7 = (f32[64,4,4]{0,2,1:T(4,128)S(1)}, f32[64,4,4]{0,2,1:T(4,128)}, u32[]{:S(2)}) copy-start(f32[64,4,4]{0,2,1:T(4,128)} %copy-done.6) | copy-start | bytes 12292
  518.5 38.3 %copy-start.9 = (f32[64,4,4]{0,2,1:T(4,128)S(1)}, f32[64,4,4]{0,2,1:T(4,128)}, u32[]{:S(2)}) copy-start(f32[64,4,4]{0,2,1:T(4,128)} %copy-done.8) | copy-start | bytes 12292
  526.7 14.4 %all-to-all-start.7 = ((bf16[4,64,4,128]{3,2,0,1:T(4,128)(2,1)}), bf16[4,64,4,128]{3,2,0,1:T(4,128)(2,1)S(1)}, u32[]{:S(2)}, u32[]{:S(2)}) async-start(bf16[4,64,4,128]{3,2,0,1:T(4,128)(2,1)} %copy.35), calls=%async_computation.7 | async-start | bytes 524288 | tf_op jit(solution)/shard_map/all_to_all | solution.py:169
  543.7 6.6 collective-permute-start.2
  546.8 7.8 collective-permute-start.6
  550.4 84.2 %collective-permute-start.3 = (bf16[7,3,64,64]{3,2,1,0:T(8,128)(2,1)S(1)}, bf16[7,3,64,64]{3,2,1,0:T(8,128)(2,1)}, u32[]{:S(2)}, u32[]{:S(2)}) collective-permute-start(bf16[7,3,64,64]{3,2,1,0:T(8,128)(2,1)S(1)} %pad_maximum_fusion.3), channel_id=1, source_target_pairs={{0,15},{1,0},{2,1},{3,2},{4,3},{5,4},{6,5},{7,6},{8,7},{9,8},{10,9... | collective-permute-start | bytes 516104 | tf_op jit(solution)/shard_map/ppermute | solution.py:16
  554.5 0.7 copy-start.2
  556.0 194.6 %collective-permute-start.7 = (bf16[7,3,64,64]{3,2,1,0:T(8,128)(2,1)}, bf16[7,3,64,64]{3,2,1,0:T(8,128)(2,1)}, u32[]{:S(2)}, u32[]{:S(2)}) collective-permute-start(bf16[7,3,64,64]{3,2,1,0:T(8,128)(2,1)} %pad_maximum_fusion.2), channel_id=1, source_target_pairs={{0,15},{1,0},{2,1},{3,2},{4,3},{5,4},{6,5},{7,6},{8,7},{9,8},{10,9... | collective-permute-start | bytes 516104 | tf_op jit(solution)/shard_map/ppermute | solution.py:16
  635.7 114.9 %copy-start.3 = (bf16[3,4,64,64]{3,2,1,0:T(8,128)(2,1)S(1)}, bf16[3,4,64,64]{3,2,1,0:T(8,128)(2,1)}, u32[]{:S(2)}) copy-start(bf16[3,4,64,64]{3,2,1,0:T(8,128)(2,1)} %copy-done.2) | copy-start | bytes 294916
  751.8 114.9 %copy-start.4 = (f32[64,512]{1,0:T(8,128)S(1)}, f32[64,512]{1,0:T(8,128)}, u32[]{:S(2)}) copy-start(f32[64,512]{1,0:T(8,128)} %fusion.161) | copy-start | bytes 393220
  866.7 9.0 %copy-start.1 = (f32[32,64]{1,0:T(8,128)S(1)}, f32[32,64]{1,0:T(8,128)}, u32[]{:S(2)}) copy-start(f32[32,64]{1,0:T(8,128)} %param.19) | copy-start | bytes 24580
where the time goes:
time: 884 us; the launch traced here: 876 us
  other arithmetic  386 us (44%)
  local copies, waits for them, and re-layouts  251 us (28%)
  blocking collectives  76.5 us (9%)
  starting transfers between devices  55.5 us (6%)
  matrix products  54.9 us (6%)
  waiting for transfers between devices  49.8 us (6%)
    scatter-add x2, other arithmetic, add_block(): return totals.at[cell_ids.reshape(-1)].add(products.reshape(-1, channels))  349 us
    gather x2, local copies, waits for them, and re-layouts, take_block(): flattened[cell_ids.reshape(-1)].reshape(64, block_len, channels)  230 us
    psum x1, blocking collectives, per_device(): filter_grad = lax.psum(partial_grad, ('slab', 'pencil'))  76.5 us
    dot_general x28, matrix products, contract(): jnp.einsum(pattern, operand, table_low, preferred_element_type=jnp.float32)  22.5 us
    dot_general x28, matrix products, contract(): jnp.einsum(pattern, operand, table_high, preferred_element_type=jnp.float32)  19.5 us
  transfers between devices with their start and end apart: 16, of which 10 were waited for; matrix products, arithmetic and copies ran while one was open for 39% of the time, Pallas kernels for 0%

commit v1 on v0

--- a/solution.py
+++ b/solution.py
@@ -203,7 +203,7 @@
     partial_grad = jnp.dot(
         shells.T, correlation.reshape(-1, C), precision=lax.Precision.HIGHEST
     ) / (N * N * N)
-    filter_grad = lax.psum(partial_grad, ("slab", "pencil"))
+    filter_grad = lax.psum(lax.psum(partial_grad, "slab"), "pencil")
     return (potential.T, charge_grad.T, filter_grad)
 
 

time: 884 us -> 923 us (1.044)
  blocking collectives: 76.5 us -> 117 us
    psum x1 -> x2, blocking collectives: 76.5 us -> 117 us  [per_device(): filter_grad = lax.psum(lax.psum(partial_grad, 'slab'), 'pencil')]
  transfers between devices with their start and end apart: 16 -> 16, of which waited for: 10 -> 10; matrix products, arithmetic and copies ran while one was open for 39% -> 37% of each run, Pallas kernels for 0% -> 0%
where the time goes in v1:
time: 923 us; the launch traced here: 915 us
  other arithmetic  386 us (42%)
  local copies, waits for them, and re-layouts  249 us (27%)
  blocking collectives  117 us (13%)
  starting transfers between devices  55.5 us (6%)
  matrix products  54.8 us (6%)
  waiting for transfers between devices  49.8 us (5%)
    scatter-add x2, other arithmetic, add_block(): return totals.at[cell_ids.reshape(-1)].add(products.reshape(-1, channels))  349 us
    gather x2, local copies, waits for them, and re-layouts, take_block(): flattened[cell_ids.reshape(-1)].reshape(64, block_len, channels)  228 us
    psum x2, blocking collectives, per_device(): filter_grad = lax.psum(lax.psum(partial_grad, 'slab'), 'pencil')  117 us
    dot_general x28, matrix products, contract(): jnp.einsum(pattern, operand, table_low, preferred_element_type=jnp.float32)  22.5 us
    dot_general x28, matrix products, contract(): jnp.einsum(pattern, operand, table_high, preferred_element_type=jnp.float32)  19.5 us
  transfers between devices with their start and end apart: 16, of which 10 were waited for; matrix products, arithmetic and copies ran while one was open for 37% of the time, Pallas kernels for 0%

profile of v1, /device:TPU:1, one launch (start us, length us, event | category | flops | bytes accessed | tf_op | source)
XLA Modules:
  0.0 915.2 jit_solution(11848298376134450899)
XLA Ops:
  6.2 12.0 %bitcast_multiply_fusion.1 = (f32[32768,64]{1,0:T(8,128)}, f32[32768,64]{1,0:T(8,128)}) fusion(f32[512,64]{1,0:T(8,128)S(1)} %copy.19, f32[32768]{0:T(1024)S(1)} %multiply_multiply_fusion, f32[512,64]{1,0:T(8,128)S(1)} %copy.28), kind=kLoop, calls=%fused_computation.9 | loop fusion | flops 4194304 | bytes 17170432 | tf_op jit(solution)/shard_map/while/body/eval_jaxpr/mul | solution.py:111
  18.2 174.7 %scatter_custom_fusion.1 = f32[3136,64]{1,0:T(8,128)S(1)} fusion(s32[32768]{0:T(1024)S(1)} %bitcast.346, f32[32768,64]{1,0:T(8,128)} %get-tuple-element.117, f32[]{:T(128)} %constant.266.clone.1), kind=kCustom, calls=%fused_computation.96 | custom fusion | flops 2097152 | bytes 803328 | tf_op jit(solution)/shard_map/while/body/eval_jaxpr/scatter-add | solution.py:112
  193.6 2.1 collective-permute-start.4
  195.7 174.7 %scatter_custom_fusion = f32[3136,64]{1,0:T(8,128)S(1)} fusion(s32[32768]{0:T(1024)S(1)} %bitcast.347, f32[32768,64]{1,0:T(8,128)} %get-tuple-element.116, f32[]{:T(128)} %constant.266.clone.1), kind=kCustom, calls=%fused_computation.98 | custom fusion | flops 2097152 | bytes 803328 | tf_op jit(solution)/shard_map/while/body/eval_jaxpr/scatter-add | solution.py:112
  371.2 1.8 collective-permute-start
  380.5 2.1 add_dynamic-update-slice_fusion
  383.6 2.8 collective-permute-start.5
  393.3 9.9 %all-to-all-start.4 = ((bf16[4,4,64,128]{3,1,0,2:T(4,128)(2,1)}), bf16[4,4,64,128]{3,1,0,2:T(4,128)(2,1)S(1)}, u32[]{:S(2)}, u32[]{:S(2)}) async-start(bf16[4,4,64,128]{3,1,0,2:T(4,128)(2,1)} %copy.29), calls=%async_computation.4 | async-start | bytes 524288 | tf_op jit(solution)/shard_map/all_to_all | solution.py:150
  406.8 8.1 all-to-all-done.4
  414.8 3.4 all-to-all-start
  421.4 8.0 all-to-all-done
  437.2 6.0 all-to-all-start.5
  447.8 3.2 all-to-all-done.5
  451.1 3.9 all-to-all-start.1
  457.3 5.1 all-to-all-done.1
  474.6 4.4 all-to-all-start.2
  479.0 1.8 convolution_subtract_fusion
  482.7 3.8 all-to-all-done.2
  486.5 3.6 all-to-all-start.6
  495.7 1.6 all-to-all-done.6
  506.9 8.0 all-to-all-start.3
  520.0 6.7 all-to-all-done.3
  526.7 3.4 all-to-all-start.7
  533.3 7.7 all-to-all-done.7
  543.7 2.3 collective-permute-start.2
  547.6 2.7 collective-permute-done.2
  551.6 2.9 collective-permute-done.6
  558.0 61.1 %psum.14 = f32[32,64]{1,0:T(8,128)S(1)} all-reduce(f32[32,64]{1,0:T(8,128)S(1)} %fusion.48), channel_id=1, replica_groups=mesh['slab'=16,'pencil'=16] {'slab'}, use_global_device_ids=true, to_apply=%region_4.5 | all-reduce | flops 2048 | bytes 16384 | tf_op jit(solution)/shard_map/psum | solution.py:206
  619.1 56.3 %psum.15 = f32[32,64]{1,0:T(8,128)} all-reduce(f32[32,64]{1,0:T(8,128)S(1)} %psum.14), channel_id=1, replica_groups=mesh['slab'=16,'pencil'=16] {'pencil'}, use_global_device_ids=true, to_apply=%region_5.6 | all-reduce | flops 2048 | bytes 16384 | tf_op jit(solution)/shard_map/psum | solution.py:206
  676.5 114.2 %gather_fusion = bf16[32768,64]{1,0:T(8,128)(2,1)} fusion(bf16[3136,64]{1,0:T(8,128)(2,1)S(1)} %bitcast.273, s32[32768]{0:T(1024)S(1)} %broadcast_clamp_fusion), kind=kCustom, calls=%fused_computation | custom fusion | bytes 8519680 | tf_op jit(solution)/shard_map/while/body/eval_jaxpr/gather | solution.py:136
  791.8 114.1 %gather_fusion.1 = bf16[32768,64]{1,0:T(8,128)(2,1)} fusion(bf16[3136,64]{1,0:T(8,128)(2,1)S(1)} %bitcast.272, s32[32768]{0:T(1024)S(1)} %broadcast_clamp_fusion), kind=kCustom, calls=%fused_computation.1 | custom fusion | bytes 8519680 | tf_op jit(solution)/shard_map/while/body/eval_jaxpr/gather | solution.py:136
  905.9 7.5 fusion
  (190 shorter events, 92.8 us)
Async XLA Ops:
  0.6 376.4 %copy-start = (f32[32,64]{1,0:T(8,128)S(1)}, f32[32,64]{1,0:T(8,128)}, u32[]{:S(2)}) copy-start(f32[32,64]{1,0:T(8,128)} %param.19) | copy-start | bytes 24580
  1.4 0.9 copy-start.10
  2.3 15.9 %copy-start.11 = (f32[512]{0:T(512)}, f32[512]{0:T(512)S(1)}, u32[]{:S(2)}) copy-start(f32[512]{0:T(512)S(1)} %fusion.301) | copy-start | bytes 6148
  6.1 189.6 %copy-start.5 = (s32[32768,1]{0,1:T(1,128)}, s32[32768,1]{0,1:T(1,128)S(1)}, u32[]{:S(2)}) copy-start(s32[32768,1]{0,1:T(1,128)S(1)} %compare_select_fusion) | copy-start | bytes 393220
  193.6 186.9 %collective-permute-start.4 = (bf16[3,7,64,64]{3,2,1,0:T(8,128)(2,1)}, bf16[3,7,64,64]{3,2,1,0:T(8,128)(2,1)}, u32[]{:S(2)}, u32[]{:S(2)}) collective-permute-start(bf16[3,7,64,64]{3,2,1,0:T(8,128)(2,1)} %bitcast.66), channel_id=1, source_target_pairs={{0,16},{16,32},{32,48},{48,64},{64,80},{80,96},{96,112},{112,128},... | collective-permute-start | bytes 516104 | tf_op jit(solution)/shard_map/ppermute | solution.py:16
  371.2 15.3 %collective-permute-start = (bf16[3,7,64,64]{3,2,1,0:T(8,128)(2,1)}, bf16[3,7,64,64]{3,2,1,0:T(8,128)(2,1)}, u32[]{:S(2)}, u32[]{:S(2)}) collective-permute-start(bf16[3,7,64,64]{3,2,1,0:T(8,128)(2,1)} %bitcast.21), channel_id=1, source_target_pairs={{0,16},{16,32},{32,48},{48,64},{64,80},{80,96},{96,112},{112,128},... | collective-permute-start | bytes 516104 | tf_op jit(solution)/shard_map/ppermute | solution.py:16
  375.9 29.1 %copy-start.13 = (f32[32]{0:T(128)}, f32[32]{0:T(128)S(1)}, u32[]{:S(2)}) copy-start(f32[32]{0:T(128)S(1)} %iota_add_fusion) | copy-start | bytes 388
  377.0 28.7 %copy-start.6 = (f32[64,4,4]{0,2,1:T(4,128)}, f32[64,4,4]{0,2,1:T(4,128)S(1)}, u32[]{:S(2)}) copy-start(f32[64,4,4]{0,2,1:T(4,128)S(1)} %get-tuple-element.128) | copy-start | bytes 12292
  377.0 28.7 %copy-start.8 = (f32[64,4,4]{0,2,1:T(4,128)}, f32[64,4,4]{0,2,1:T(4,128)S(1)}, u32[]{:S(2)}) copy-start(f32[64,4,4]{0,2,1:T(4,128)S(1)} %get-tuple-element.129) | copy-start | bytes 12292
  383.6 6.1 collective-permute-start.5
  388.9 14.4 %collective-permute-start.1 = (bf16[4,3,64,64]{3,2,1,0:T(8,128)(2,1)S(1)}, bf16[4,3,64,64]{3,2,1,0:T(8,128)(2,1)}, u32[]{:S(2)}, u32[]{:S(2)}) collective-permute-start(bf16[4,3,64,64]{3,2,1,0:T(8,128)(2,1)S(1)} %slice.473), channel_id=1, source_target_pairs={{0,1},{1,2},{2,3},{3,4},{4,5},{5,6},{6,7},{7,8},{8,9},{9,10},{10,1... | collective-permute-start | bytes 294920 | tf_op jit(solution)/shard_map/ppermute | solution.py:16
  393.3 21.5 %all-to-all-start.4 = ((bf16[4,4,64,128]{3,1,0,2:T(4,128)(2,1)}), bf16[4,4,64,128]{3,1,0,2:T(4,128)(2,1)S(1)}, u32[]{:S(2)}, u32[]{:S(2)}) async-start(bf16[4,4,64,128]{3,1,0,2:T(4,128)(2,1)} %copy.29), calls=%async_computation.4 | async-start | bytes 524288 | tf_op jit(solution)/shard_map/all_to_all | solution.py:150
  414.8 14.6 %all-to-all-start = ((bf16[4,4,64,128]{3,1,0,2:T(4,128)(2,1)}), bf16[4,4,64,128]{3,1,0,2:T(4,128)(2,1)S(1)}, u32[]{:S(2)}, u32[]{:S(2)}) async-start(bf16[4,4,64,128]{3,1,0,2:T(4,128)(2,1)} %copy.20), calls=%async_computation | async-start | bytes 524288 | tf_op jit(solution)/shard_map/all_to_all | solution.py:150
  437.2 13.9 %all-to-all-start.5 = ((bf16[4,64,4,128]{3,2,0,1:T(4,128)(2,1)}), bf16[4,64,4,128]{3,2,0,1:T(4,128)(2,1)S(1)}, u32[]{:S(2)}, u32[]{:S(2)}) async-start(bf16[4,64,4,128]{3,2,0,1:T(4,128)(2,1)} %copy.31), calls=%async_computation.5 | async-start | bytes 524288 | tf_op jit(solution)/shard_map/all_to_all | solution.py:155
  451.1 11.3 %all-to-all-start.1 = ((bf16[4,64,4,128]{3,2,0,1:T(4,128)(2,1)}), bf16[4,64,4,128]{3,2,0,1:T(4,128)(2,1)S(1)}, u32[]{:S(2)}, u32[]{:S(2)}) async-start(bf16[4,64,4,128]{3,2,0,1:T(4,128)(2,1)} %copy.22), calls=%async_computation.1 | async-start | bytes 524288 | tf_op jit(solution)/shard_map/all_to_all | solution.py:155
  474.6 11.9 %all-to-all-start.2 = ((bf16[64,4,4,128]{3,2,1,0:T(4,128)(2,1)}), bf16[64,4,4,128]{3,2,1,0:T(4,128)(2,1)}, u32[]{:S(2)}, u32[]{:S(2)}) async-start(bf16[64,4,4,128]{3,2,1,0:T(4,128)(2,1)} %copy.24), calls=%async_computation.2 | async-start | bytes 524288 | tf_op jit(solution)/shard_map/all_to_all | solution.py:164
  486.5 10.9 %all-to-all-start.6 = ((bf16[64,4,4,128]{3,2,1,0:T(4,128)(2,1)}), bf16[64,4,4,128]{3,2,1,0:T(4,128)(2,1)S(1)}, u32[]{:S(2)}, u32[]{:S(2)}) async-start(bf16[64,4,4,128]{3,2,1,0:T(4,128)(2,1)} %copy.33), calls=%async_computation.6 | async-start | bytes 524288 | tf_op jit(solution)/shard_map/all_to_all | solution.py:164
  501.5 28.6 %copy-start.12 = (f32[512]{0:T(512)S(1)}, f32[512]{0:T(512)}, u32[]{:S(2)}) copy-start(f32[512]{0:T(512)} %copy-done.11) | copy-start | bytes 6148
  506.9 19.8 %all-to-all-start.3 = ((bf16[4,64,4,128]{3,2,0,1:T(4,128)(2,1)}), bf16[4,64,4,128]{3,2,0,1:T(4,128)(2,1)S(1)}, u32[]{:S(2)}, u32[]{:S(2)}) async-start(bf16[4,64,4,128]{3,2,0,1:T(4,128)(2,1)} %copy.26), calls=%async_computation.3 | async-start | bytes 524288 | tf_op jit(solution)/shard_map/all_to_all | solution.py:169
  518.4 38.4 %copy-start.7 = (f32[64,4,4]{0,2,1:T(4,128)S(1)}, f32[64,4,4]{0,2,1:T(4,128)}, u32[]{:S(2)}) copy-start(f32[64,4,4]{0,2,1:T(4,128)} %copy-done.6) | copy-start | bytes 12292
  518.5 38.3 %copy-start.9 = (f32[64,4,4]{0,2,1:T(4,128)S(1)}, f32[64,4,4]{0,2,1:T(4,128)}, u32[]{:S(2)}) copy-start(f32[64,4,4]{0,2,1:T(4,128)} %copy-done.8) | copy-start | bytes 12292
  526.7 14.4 %all-to-all-start.7 = ((bf16[4,64,4,128]{3,2,0,1:T(4,128)(2,1)}), bf16[4,64,4,128]{3,2,0,1:T(4,128)(2,1)S(1)}, u32[]{:S(2)}, u32[]{:S(2)}) async-start(bf16[4,64,4,128]{3,2,0,1:T(4,128)(2,1)} %copy.35), calls=%async_computation.7 | async-start | bytes 524288 | tf_op jit(solution)/shard_map/all_to_all | solution.py:169
  543.7 6.6 collective-permute-start.2
  546.7 7.8 collective-permute-start.6
  550.4 125.0 %collective-permute-start.3 = (bf16[7,3,64,64]{3,2,1,0:T(8,128)(2,1)S(1)}, bf16[7,3,64,64]{3,2,1,0:T(8,128)(2,1)}, u32[]{:S(2)}, u32[]{:S(2)}) collective-permute-start(bf16[7,3,64,64]{3,2,1,0:T(8,128)(2,1)S(1)} %pad_maximum_fusion.3), channel_id=1, source_target_pairs={{0,15},{1,0},{2,1},{3,2},{4,3},{5,4},{6,5},{7,6},{8,7},{9,8},{10,9... | collective-permute-start | bytes 516104 | tf_op jit(solution)/shard_map/ppermute | solution.py:16
  554.5 0.7 copy-start.2
  556.0 234.7 %collective-permute-start.7 = (bf16[7,3,64,64]{3,2,1,0:T(8,128)(2,1)}, bf16[7,3,64,64]{3,2,1,0:T(8,128)(2,1)}, u32[]{:S(2)}, u32[]{:S(2)}) collective-permute-start(bf16[7,3,64,64]{3,2,1,0:T(8,128)(2,1)} %pad_maximum_fusion.2), channel_id=1, source_target_pairs={{0,15},{1,0},{2,1},{3,2},{4,3},{5,4},{6,5},{7,6},{8,7},{9,8},{10,9... | collective-permute-start | bytes 516104 | tf_op jit(solution)/shard_map/ppermute | solution.py:16
  676.5 114.2 %copy-start.3 = (bf16[3,4,64,64]{3,2,1,0:T(8,128)(2,1)S(1)}, bf16[3,4,64,64]{3,2,1,0:T(8,128)(2,1)}, u32[]{:S(2)}) copy-start(bf16[3,4,64,64]{3,2,1,0:T(8,128)(2,1)} %copy-done.2) | copy-start | bytes 294916
  791.8 114.1 %copy-start.4 = (f32[64,512]{1,0:T(8,128)S(1)}, f32[64,512]{1,0:T(8,128)}, u32[]{:S(2)}) copy-start(f32[64,512]{1,0:T(8,128)} %fusion.161) | copy-start | bytes 393220
  905.9 9.0 copy-start.1
